TPU v7x, 32 devices: a whole 2x2x4 slice. The times are simulated.
32 devices in a mesh: rep: 4 (over z), fsdp: 2 (over x), seq: 4 (over y, core).
Axes of the slice: x: 2, y: 2, z: 4, core: 2. Of those that a mesh axis runs over, the one named last changes fastest.
Arguments:
- tokens: bfloat16 [8, 1024, 640], P(('rep', 'fsdp'), 'seq'), may hold values from -6 to 6
- d_out: bfloat16 [8, 1024, 640], P(('rep', 'fsdp'), 'seq'), may hold values from -6 to 6
- doc_lengths: int32 [8, 3], P(('rep', 'fsdp')), may hold values from 1 to 640, 1024 in all within a row
- w_query: bfloat16 [640, 1024], P('fsdp'), may hold values from -0.25 to 0.25
- w_key: bfloat16 [640, 256], P('fsdp'), may hold values from -0.25 to 0.25
- w_value: bfloat16 [640, 256], P('fsdp'), may hold values from -0.25 to 0.25
- w_out: bfloat16 [1024, 640], P('fsdp'), may hold values from -0.1875 to 0.1875
- w_gate: bfloat16 [640, 2048], P('fsdp'), may hold values from -0.25 to 0.25
- w_up: bfloat16 [640, 2048], P('fsdp'), may hold values from -0.25 to 0.25
- w_down: bfloat16 [2048, 640], P('fsdp'), may hold values from -0.125 to 0.125
- g_input: bfloat16 [640], P('fsdp'), may hold values from 0.5 to 1.5
- g_query: bfloat16 [256], P('fsdp'), may hold values from 0.25 to 1.75
- g_key: bfloat16 [256], P('fsdp'), may hold values from 0.25 to 1.75
- g_attn: bfloat16 [640], P('fsdp'), may hold values from 0.5 to 1.5
- g_ffin: bfloat16 [640], P('fsdp'), may hold values from 0.5 to 1.5
- g_ffout: bfloat16 [640], P('fsdp'), may hold values from 0.5 to 1.5
Outputs:
- result: bfloat16 [8, 1024, 640], P(('rep', 'fsdp'), 'seq')
- d_tokens: bfloat16 [8, 1024, 640], P(('rep', 'fsdp'), 'seq')
- grad_query: float32 [640, 1024], P('fsdp')
- grad_key: float32 [640, 256], P('fsdp')
- grad_value: float32 [640, 256], P('fsdp')
- grad_out: float32 [1024, 640], P('fsdp')
- grad_gate: float32 [640, 2048], P('fsdp')
- grad_up: float32 [640, 2048], P('fsdp')
- grad_down: float32 [2048, 640], P('fsdp')
- grad_ginput: float32 [640], P('fsdp')
- grad_gquery: float32 [256], P('fsdp')
- grad_gkey: float32 [256], P('fsdp')
- grad_gattn: float32 [640], P('fsdp')
- grad_gffin: float32 [640], P('fsdp')
- grad_gffout: float32 [640], P('fsdp')
Inputs may be any that keep to these rules, and one draw needn't show every extreme that they name: `doc_lengths`: each row lists the lengths of the 3 documents packed in order into one sequence; a row sums to 1024 and its largest entry is 640.
All inputs are finite; a program needn't handle non-finite values.
Results may differ from a plain program's by a relative error of at most 0.024.
Values may be sent and summed in bfloat16 or wider, within the bound.
A program may use at most 128 MiB of HBM per device.

v0:
```python
import jax
import jax.numpy as jnp
from jax import lax
from jax.sharding import PartitionSpec as P

EPS = 1e-06
ROPE_BASE = 1000000.0
MASKED = -1e30


def rms_norm(values, gain_vec):
    return values * lax.rsqrt(jnp.mean(values * values, axis=-1, keepdims=True) + EPS) * gain_vec


def rotate(values, angles):
    half_width = values.shape[-1] // 2
    front_half = values[..., :half_width]
    back_half = values[..., half_width:]
    cos_part = jnp.cos(angles)
    sin_part = jnp.sin(angles)
    return jnp.concatenate(
        [
            front_half * cos_part - back_half * sin_part,
            back_half * cos_part + front_half * sin_part,
        ],
        axis=-1,
    )


def frequencies(head_size):
    return jnp.power(
        jnp.float32(ROPE_BASE), -2.0 * jnp.arange(head_size // 2, dtype=jnp.float32) / head_size
    )


def layout(lengths_row, total_len):
    doc_ends = jnp.cumsum(lengths_row)
    starts = doc_ends - lengths_row
    indices = jnp.arange(total_len, dtype=jnp.int32)
    segment = jnp.sum((indices[:, None] >= doc_ends[None, :]).astype(jnp.int32), axis=1)
    onehot = segment[:, None] == jnp.arange(lengths_row.shape[0], dtype=jnp.int32)[None, :]
    doc_begin = jnp.sum(jnp.where(onehot, starts[None, :], 0), axis=1)
    return (segment, indices - doc_begin)


def matmul(left_side, right_side):
    return jnp.dot(left_side, right_side, preferred_element_type=jnp.float32)


def times_transpose(left_side, right_side):
    return lax.dot_general(
        left_side, right_side, (((1,), (1,)), ((), ())), preferred_element_type=jnp.float32
    )


def transpose_times(left_side, right_side):
    return lax.dot_general(
        left_side, right_side, (((0,), (0,)), ((), ())), preferred_element_type=jnp.float32
    )


def gated(gate_proj, up_proj):
    return jax.nn.gelu(gate_proj, approximate=True) * up_proj


def swap(values, axis_name, bit):
    size = lax.axis_size(axis_name)
    return lax.ppermute(values, axis_name, [(i, i ^ bit) for i in range(size)])


def halve(values, axis_name, bit, dim):
    mine = lax.axis_index(axis_name) // bit % 2
    sent = lax.dynamic_index_in_dim(values, 1 - mine, dim, keepdims=False)
    kept = lax.dynamic_index_in_dim(values, mine, dim, keepdims=False)
    arrived = swap(sent, axis_name, bit)
    return (kept.astype(jnp.float32) + arrived.astype(jnp.float32)).astype(jnp.bfloat16)


def paired():
    return lax.axis_size("fsdp") == 2 and lax.axis_size("seq") == 4


def gather_rows(shard):
    if not paired():
        return lax.all_gather(shard, "fsdp", axis=0, tiled=True)
    rows = shard.shape[0] // 4
    piece = lax.dynamic_slice_in_dim(shard, lax.axis_index("seq") * rows, rows)
    other = lax.all_gather(swap(piece, "fsdp", 1), "seq", axis=0, tiled=True)
    first = lax.axis_index("fsdp") == 0
    return jnp.concatenate([jnp.where(first, shard, other), jnp.where(first, other, shard)], axis=0)


def reduce_blocks(blocks, across_first, before):
    _, _, rows, columns = blocks.shape
    part = blocks.reshape(2, 2, 2, rows, columns)
    part = halve(part, "seq", 1, 2)
    if across_first:
        part = halve(part, "fsdp", 1, 0)
        part = halve(part, "seq", 2, 0)
    else:
        part = halve(part, "seq", 2, 1)
        part = halve(part, "fsdp", 1, 0)
    if before is not None:
        part, _ = lax.optimization_barrier((part, before))
    part = lax.psum(part, "rep")
    return (lax.all_gather(part, "seq", axis=0, tiled=True).reshape(4, rows, columns), part)


def reduce_rows(grad, across_first, before):
    low = grad.astype(jnp.bfloat16)
    if not paired():
        own = lax.psum_scatter(low, "fsdp", scatter_dimension=0, tiled=True)
        return (lax.psum(own, ("rep", "seq")).astype(jnp.float32), None)
    rows, columns = low.shape
    own, last = reduce_blocks(low.reshape(2, 4, rows // 8, columns), across_first, before)
    return (own.reshape(rows // 2, columns).astype(jnp.float32), last)


def reduce_with_gains(grad, gains, before):
    width = gains.shape[1]
    rows, columns = grad.shape
    if not paired() or width > columns:
        own = lax.psum_scatter(gains.astype(jnp.bfloat16), "fsdp", scatter_dimension=0, tiled=True)
        own = lax.psum(own, ("rep", "seq")).astype(jnp.float32)
        return (reduce_rows(grad, True, before)[0], own[0])
    extra = jnp.pad(
        gains.astype(jnp.bfloat16)[:, None, None, :],
        ((0, 0), (0, 3), (0, 15), (0, columns - width)),
    )
    blocks = jnp.concatenate(
        [grad.astype(jnp.bfloat16).reshape(2, 4, rows // 8, columns), extra], axis=2
    )
    own, _ = reduce_blocks(blocks, True, before)
    matrix = own[:, : rows // 8].reshape(rows // 2, columns).astype(jnp.float32)
    return (matrix, own[0, rows // 8, :width].astype(jnp.float32))


def body(
    tokens,
    d_out,
    doc_lengths,
    w_query,
    w_key,
    w_value,
    w_out,
    w_gate,
    w_up,
    w_down,
    g_input,
    g_query,
    g_key,
    g_attn,
    g_ffin,
    g_ffout,
):
    shards = lax.axis_size("fsdp")
    gain_shards = (g_input, g_query, g_key, g_attn, g_ffin, g_ffout)
    widths = [entry.shape[0] for entry in gain_shards]
    starts = [sum(widths[:i]) for i in range(len(widths))]
    gain_rows = lax.all_gather(jnp.concatenate(gain_shards)[None], "fsdp", axis=0, tiled=True)
    gain_input, gain_query, gain_key, gain_attn, gain_ffin, gain_ffout = [
        gain_rows[:, at : at + width].reshape(-1).astype(jnp.float32)
        for at, width in zip(starts, widths)
    ]
    qkv_mat = gather_rows(jnp.concatenate([w_query, w_key, w_value], axis=1))
    out_mat = gather_rows(w_out)
    gate_up_mat = gather_rows(jnp.concatenate([w_gate, w_up], axis=1))
    down_mat = gather_rows(w_down)
    row_count = tokens.shape[1]
    head_size = gain_query.shape[0]
    query_width = w_query.shape[1]
    head_count = query_width // head_size
    ff_width = w_gate.shape[1]
    total_len = row_count * lax.axis_size("seq")
    segment, position = layout(doc_lengths[0], total_len)
    offset = lax.axis_index("seq") * row_count
    query_seg = lax.dynamic_slice_in_dim(segment, offset, row_count)
    query_pos = lax.dynamic_slice_in_dim(position, offset, row_count)
    places = offset + jnp.arange(row_count, dtype=jnp.int32)
    allowed = (query_seg[:, None] == segment[None, :]) & (
        places[:, None] >= jnp.arange(total_len, dtype=jnp.int32)[None, :]
    )
    angles = query_pos.astype(jnp.float32)[:, None] * frequencies(head_size)[None, :]
    scaling = head_size ** (-0.5)
    inputs = tokens[0].astype(jnp.float32)
    cotangent = d_out[0].astype(jnp.float32)
    input_norm, input_pull = jax.vjp(rms_norm, inputs, gain_input)
    attn_input = input_norm.astype(jnp.bfloat16)
    qkv_proj = matmul(attn_input, qkv_mat)
    q_proj = qkv_proj[:, :query_width]
    k_proj = qkv_proj[:, query_width : query_width + head_size]
    v_proj = qkv_proj[:, query_width + head_size :]

    def query_fn(projected, gain_vec):
        shaped = projected.reshape(projected.shape[0], -1, gain_vec.shape[0])
        return rotate(rms_norm(shaped, gain_vec), angles[:, None, :])

    def key_fn(projected, gain_vec):
        return rotate(rms_norm(projected, gain_vec), angles)

    queries, query_pull = jax.vjp(query_fn, q_proj, gain_query)
    keys_own, key_pull = jax.vjp(key_fn, k_proj, gain_key)
    query_rows = queries.astype(jnp.bfloat16).reshape(row_count * head_count, head_size)
    key_value_rows = lax.all_gather(
        jnp.concatenate([keys_own.astype(jnp.bfloat16), v_proj.astype(jnp.bfloat16)], axis=1),
        "seq",
        axis=0,
        tiled=True,
    )
    key_rows = key_value_rows[:, :head_size]
    value_rows = key_value_rows[:, head_size:]

    def masked_scores():
        raw_scores = times_transpose(query_rows, key_rows).reshape(row_count, head_count, total_len)
        return jnp.where(allowed[:, None, :], raw_scores * scaling, MASKED)

    scores = masked_scores()
    top_score = jnp.max(scores, axis=-1, keepdims=True)
    shifted = jnp.exp(scores - top_score)
    denominator = jnp.sum(shifted, axis=-1, keepdims=True)
    log_total = top_score + jnp.log(denominator)
    probs_low = (
        (shifted / denominator).astype(jnp.bfloat16).reshape(row_count * head_count, total_len)
    )
    mixed_rows = (
        matmul(probs_low, value_rows)
        .reshape(row_count, head_count * head_size)
        .astype(jnp.bfloat16)
    )
    out_proj = matmul(mixed_rows, out_mat)
    attn_norm, attn_pull = jax.vjp(rms_norm, out_proj, gain_attn)
    hidden_one = inputs + attn_norm
    ffin_norm, ffin_pull = jax.vjp(rms_norm, hidden_one, gain_ffin)
    ff_input = ffin_norm.astype(jnp.bfloat16)
    gate_up_proj = matmul(ff_input, gate_up_mat)
    gate_proj = gate_up_proj[:, :ff_width]
    up_proj = gate_up_proj[:, ff_width:]
    activated, gated_pull = jax.vjp(gated, gate_proj, up_proj)
    hidden = activated.astype(jnp.bfloat16)
    down_proj = matmul(hidden, down_mat)
    ffout_norm, ffout_pull = jax.vjp(rms_norm, down_proj, gain_ffout)
    result = hidden_one + ffout_norm
    d_down, grad_gffout = ffout_pull(cotangent)
    d_down_low = d_down.astype(jnp.bfloat16)
    total_down, last = reduce_rows(transpose_times(hidden, d_down_low), True, None)
    d_hidden = times_transpose(d_down_low, down_mat)
    d_gate, d_up = gated_pull(d_hidden)
    d_gate_up_low = jnp.concatenate(
        [d_gate.astype(jnp.bfloat16), d_up.astype(jnp.bfloat16)], axis=1
    )
    total_gate_up, last = reduce_rows(transpose_times(ff_input, d_gate_up_low), False, last)
    d_ffin = times_transpose(d_gate_up_low, gate_up_mat)
    d_hidden_part, grad_gffin = ffin_pull(d_ffin)
    d_hidden_one = cotangent + d_hidden_part
    d_out_proj, grad_gattn = attn_pull(d_hidden_one)
    d_out_low = d_out_proj.astype(jnp.bfloat16)
    total_out, last = reduce_rows(transpose_times(mixed_rows, d_out_low), True, last)
    d_mixed = (
        times_transpose(d_out_low, out_mat)
        .astype(jnp.bfloat16)
        .reshape(row_count * head_count, head_size)
    )
    probs_full = jnp.exp(masked_scores() - log_total)
    d_probs = times_transpose(d_mixed, value_rows).reshape(row_count, head_count, total_len)
    row_dot = jnp.sum(probs_full * d_probs, axis=-1, keepdims=True)
    d_raw = (
        (probs_full * (d_probs - row_dot) * scaling)
        .astype(jnp.bfloat16)
        .reshape(row_count * head_count, total_len)
    )
    grad_rows = jnp.concatenate(
        [
            transpose_times(d_raw, query_rows).astype(jnp.bfloat16),
            transpose_times(probs_low, d_mixed).astype(jnp.bfloat16),
        ],
        axis=1,
    )
    d_queries = matmul(d_raw, key_rows).reshape(row_count, head_count, head_size)
    if paired():
        grad_own = grad_rows.reshape(2, 2, row_count, 2 * head_size)
        grad_own = halve(halve(grad_own, "seq", 1, 1), "seq", 2, 0).astype(jnp.float32)
    else:
        grad_own = lax.psum_scatter(grad_rows, "seq", scatter_dimension=0, tiled=True).astype(
            jnp.float32
        )
    d_q_proj, grad_gquery = query_pull(d_queries)
    d_k_proj, grad_gkey = key_pull(grad_own[:, :head_size])
    d_qkv_low = jnp.concatenate(
        [
            d_q_proj.astype(jnp.bfloat16),
            d_k_proj.astype(jnp.bfloat16),
            grad_own[:, head_size:].astype(jnp.bfloat16),
        ],
        axis=1,
    )
    d_qkv_low, last, total_down = lax.optimization_barrier((d_qkv_low, last, total_down))
    grad_qkv = transpose_times(attn_input, d_qkv_low)
    d_attn_input = times_transpose(d_qkv_low, qkv_mat)
    d_inputs_part, grad_ginput = input_pull(d_attn_input)
    d_inputs = d_hidden_one + d_inputs_part
    grad_gains = (grad_ginput, grad_gquery, grad_gkey, grad_gattn, grad_gffin, grad_gffout)
    packed_gains = jnp.concatenate([entry.reshape(shards, -1) for entry in grad_gains], axis=1)
    total_qkv, total_gains = reduce_with_gains(grad_qkv, packed_gains, last)
    return (
        result.astype(jnp.bfloat16)[None],
        d_inputs.astype(jnp.bfloat16)[None],
        total_qkv[:, :query_width],
        total_qkv[:, query_width : query_width + head_size],
        total_qkv[:, query_width + head_size :],
        total_out,
        total_gate_up[:, :ff_width],
        total_gate_up[:, ff_width:],
        total_down,
    ) + tuple((total_gains[at : at + width] for at, width in zip(starts, widths)))


def solution(mesh):
    in_specs = (
        P(("rep", "fsdp"), "seq", None),
        P(("rep", "fsdp"), "seq", None),
        P(("rep", "fsdp"), None),
        P("fsdp", None),
        P("fsdp", None),
        P("fsdp", None),
        P("fsdp", None),
        P("fsdp", None),
        P("fsdp", None),
        P("fsdp", None),
        P("fsdp"),
        P("fsdp"),
        P("fsdp"),
        P("fsdp"),
        P("fsdp"),
        P("fsdp"),
    )
    out_specs = (
        P(("rep", "fsdp"), "seq", None),
        P(("rep", "fsdp"), "seq", None),
        P("fsdp", None),
        P("fsdp", None),
        P("fsdp", None),
        P("fsdp", None),
        P("fsdp", None),
        P("fsdp", None),
        P("fsdp", None),
        P("fsdp"),
        P("fsdp"),
        P("fsdp"),
        P("fsdp"),
        P("fsdp"),
        P("fsdp"),
    )
    return jax.shard_map(body, mesh=mesh, in_specs=in_specs, out_specs=out_specs, check_vma=False)
```

profile of v0, /device:TPU:0, one launch (start us, length us, event | category | flops | bytes accessed | tf_op | source)
XLA Modules:
  0.0 461.6 jit_solution(1109950288446582475)
XLA Ops:
  10.4 3.0 collective-permute-start
  14.1 5.5 %all-gather.1 = bf16[2,1,1536]{2,1,0:T(2,128)(2,1)S(1)} all-gather(bf16[1,1,1536]{2,1,0:T(2,128)(2,1)S(1)} %reshape.530), channel_id=2, replica_groups=mesh['rep'=4,'fsdp'=2,'seq'=4] {'fsdp'}, dimensions={0}, use_global_device_ids=true | all-gather | bytes 9216 | tf_op jit(solution)/shard_map/all_gather | solution.py:160
  20.0 9.9 %all_gather.31 = bf16[320,1536]{1,0:T(8,128)(2,1)S(1)} all-gather(bf16[80,1536]{1,0:T(8,128)(2,1)S(1)} %collective-permute-done), channel_id=1, replica_groups=mesh['rep'=4,'fsdp'=2,'seq'=4] {'seq'}, dimensions={0}, use_global_device_ids=true | all-gather | bytes 1228800 | tf_op jit(solution)/shard_map/all_gather | solution.py:88
  36.3 8.7 %collective-permute-done.3 = bf16[256,640]{1,0:T(8,128)(2,1)S(1)} collective-permute-done((bf16[256,640]{1,0:T(8,128)(2,1)}, bf16[256,640]{1,0:T(8,128)(2,1)S(1)}, u32[]{:S(2)}, u32[]{:S(2)}) %collective-permute-start.3) | collective-permute-done | bytes 327712 | tf_op jit(solution)/shard_map/ppermute | solution.py:68
  54.6 6.8 %all_gather.33 = bf16[512,640]{1,0:T(8,128)(2,1)S(1)} all-gather(bf16[128,640]{1,0:T(8,128)(2,1)S(1)} %collective-permute-done.1), channel_id=1, replica_groups=mesh['rep'=4,'fsdp'=2,'seq'=4] {'seq'}, dimensions={0}, use_global_device_ids=true | all-gather | bytes 819200 | tf_op jit(solution)/shard_map/all_gather | solution.py:88
  63.2 5.7 %collective-permute-done.2 = bf16[80,4096]{1,0:T(8,128)(2,1)} collective-permute-done((bf16[80,4096]{1,0:T(8,128)(2,1)}, bf16[80,4096]{1,0:T(8,128)(2,1)}, u32[]{:S(2)}, u32[]{:S(2)}) %collective-permute-start.2) | collective-permute-done | bytes 655392 | tf_op jit(solution)/shard_map/ppermute | solution.py:68
  69.9 2.1 fusion.126
  75.6 2.6 reshape.502
  78.2 2.7 convolution_convert_fusion.6
  81.2 1.9 multiply_reduce_fusion.9
  83.5 3.4 broadcast_select_fusion.3
  86.9 10.6 %all-gather.11.cloned.1.call-done = bf16[320,4096]{1,0:T(8,128)(2,1)} async-done(((bf16[80,4096]{1,0:T(8,128)(2,1)}), bf16[320,4096]{1,0:T(8,128)(2,1)}) %all-gather.11.cloned.1.call-update) | async-done | bytes 2621456 | tf_op jit(solution)/shard_map/all_gather | solution.py:88
  97.6 2.9 broadcast_select_fusion.1
  100.5 1.9 fusion.5
  106.5 4.6 %fusion.23 = (bf16[256,2048]{1,0:T(8,128)(2,1)S(1)}, bf16[256,2048]{1,0:T(8,128)(2,1)S(1)}) fusion(f32[256,4096]{1,0:T(8,128)S(1)} %fusion.5, bf16[256,640]{1,0:T(8,128)(2,1)S(1)} %get-tuple-element.64, bf16[1024,640]{1,0:T(8,128)(2,1)S(1)} %copy-done.23, bf16[1024,640]{1,0:T(8,128)(2,1)S(1)} %copy-done.22), kind=kOutput, calls=%fused_computation.42 | convolution fusion | flops 688914432 | bytes 9240576 | tf_op jit(solution)/shard_map/dot_general | solution.py:51
  111.2 2.1 multiply_reduce_fusion.3
  115.0 2.1 constant_dynamic-slice_fusion.1
  123.0 1.9 convolution_convert_fusion.3
  130.0 2.8 fusion.71
  132.8 12.5 %fusion.38 = bf16[1024,256]{0,1:T(8,128)(2,1)} fusion(f32[256,4,1024]{2,0,1:T(8,128)} %fusion.71, f32[256,4,1024]{2,0,1:T(8,128)} %copy-done, f32[256,4]{0,1:T(4,128)S(1)} %log_add_fusion, bf16[256,4,128]{2,0,1:T(8,128)(2,1)} %copy-done.42, bf16[256,4,128]{2,0,1:T(8,128)(2,1)} %copy-done.41), kind=kOutput, calls=%fused_computation.73 | convolution fusion | flops 545523712 | bytes 9441280 | tf_op jit(solution)/shard_map/dot_general | solution.py:57
  145.3 2.6 convolution_convert_fusion.4
  147.9 2.9 fusion.1
  159.4 2.3 copy.140
  161.7 12.3 %fusion.15 = f32[256,4,256]{2,0,1:T(8,128)} fusion(f32[256,4,1024]{2,0,1:T(8,128)} %fusion.71, f32[256,4,1024]{2,0,1:T(8,128)} %copy-done, f32[256,4]{0,1:T(4,128)S(1)} %log_add_fusion, bf16[1024,512]{1,0:T(8,128)(2,1)} %all-gather.9.cloned.1.call-done), kind=kOutput, calls=%fused_computation.33 | convolution fusion | flops 544212992 | bytes 18358272 | tf_op jit(solution)/shard_map/dot_general | solution.py:47
  177.4 5.9 %collective-permute-done.10 = bf16[2,80,4096]{2,1,0:T(8,128)(2,1)} collective-permute-done((bf16[2,80,4096]{2,1,0:T(8,128)(2,1)}, bf16[2,80,4096]{2,1,0:T(8,128)(2,1)}, u32[]{:S(2)}, u32[]{:S(2)}) %collective-permute-start.10) | collective-permute-done | bytes 1310752 | tf_op jit(solution)/shard_map/ppermute | solution.py:68
  190.4 6.9 %collective-permute-done.14 = bf16[256,640]{1,0:T(8,128)(2,1)S(1)} collective-permute-done((bf16[256,640]{1,0:T(8,128)(2,1)S(1)}, bf16[256,640]{1,0:T(8,128)(2,1)S(1)}, u32[]{:S(2)}, u32[]{:S(2)}) %collective-permute-start.14) | collective-permute-done | bytes 327712 | tf_op jit(solution)/shard_map/ppermute | solution.py:68
  198.2 5.2 %collective-permute-done.11 = bf16[80,4096]{1,0:T(8,128)(2,1)} collective-permute-done((bf16[80,4096]{1,0:T(8,128)(2,1)}, bf16[80,4096]{1,0:T(8,128)(2,1)}, u32[]{:S(2)}, u32[]{:S(2)}) %collective-permute-start.11) | collective-permute-done | bytes 655392 | tf_op jit(solution)/shard_map/ppermute | solution.py:68
  203.4 2.3 fusion.36
  205.7 28.2 %all-reduce.10.cloned.1.call-done = bf16[256,640]{1,0:T(8,128)(2,1)} async-done(((bf16[256,640]{1,0:T(8,128)(2,1)}), bf16[256,640]{1,0:T(8,128)(2,1)}) %all-reduce.10.cloned.1.call-update) | async-done | bytes 327696 | tf_op jit(solution)/shard_map/psum | solution.py:105
  234.2 2.3 fusion.48
  236.5 2.0 copy.138
  244.4 2.0 collective-permute-done.5
  248.2 2.0 collective-permute-done.7
  252.9 2.8 collective-permute-done.8
  256.4 20.6 %all-reduce.12.cloned.1.call-done = bf16[80,4096]{1,0:T(8,128)(2,1)} async-done(((bf16[80,4096]{1,0:T(8,128)(2,1)}), bf16[80,4096]{1,0:T(8,128)(2,1)}) %all-reduce.12.cloned.1.call-update) | async-done | bytes 655376 | tf_op jit(solution)/shard_map/psum | solution.py:105
  278.1 18.0 %all-gather.15.cloned.1.call-done = bf16[1024,640]{1,0:T(8,128)(2,1)} async-done(((bf16[256,640]{1,0:T(8,128)(2,1)}), bf16[1024,640]{1,0:T(8,128)(2,1)}) %all-gather.15.cloned.1.call-update) | async-done | bytes 1310736 | tf_op jit(solution)/shard_map/all_gather | solution.py:106
  296.1 3.0 convert_element_type.437
  299.1 34.8 %all-reduce.14.cloned.1.call-done = bf16[128,640]{1,0:T(8,128)(2,1)} async-done(((bf16[128,640]{1,0:T(8,128)(2,1)}), bf16[128,640]{1,0:T(8,128)(2,1)}) %all-reduce.14.cloned.1.call-update) | async-done | bytes 163856 | tf_op jit(solution)/shard_map/psum | solution.py:105
  333.9 2.9 fusion.59
  336.8 2.0 convolution_convert_fusion.2
  339.4 2.8 collective-permute-done.15
  344.1 13.9 %collective-permute-done.16 = bf16[2,96,1536]{2,1,0:T(8,128)(2,1)S(1)} collective-permute-done((bf16[2,96,1536]{2,1,0:T(8,128)(2,1)S(1)}, bf16[2,96,1536]{2,1,0:T(8,128)(2,1)S(1)}, u32[]{:S(2)}, u32[]{:S(2)}) %collective-permute-start.16) | collective-permute-done | bytes 589856 | tf_op jit(solution)/shard_map/ppermute | solution.py:68
  359.7 6.8 %collective-permute-done.17 = bf16[96,1536]{1,0:T(8,128)(2,1)S(1)} collective-permute-done((bf16[96,1536]{1,0:T(8,128)(2,1)S(1)}, bf16[96,1536]{1,0:T(8,128)(2,1)S(1)}, u32[]{:S(2)}, u32[]{:S(2)}) %collective-permute-start.17) | collective-permute-done | bytes 294944 | tf_op jit(solution)/shard_map/ppermute | solution.py:68
  368.1 35.0 %all-reduce.16.cloned.1.call-done = bf16[96,1536]{1,0:T(8,128)(2,1)} async-done(((bf16[96,1536]{1,0:T(8,128)(2,1)}), bf16[96,1536]{1,0:T(8,128)(2,1)}) %all-reduce.16.cloned.1.call-update) | async-done | bytes 294928 | tf_op jit(solution)/shard_map/psum | solution.py:105
  403.1 7.9 %all_gather.38 = bf16[512,640]{1,0:T(8,128)(2,1)S(1)} all-gather(bf16[128,640]{1,0:T(8,128)(2,1)S(1)} %copy-done.44), channel_id=1, replica_groups=mesh['rep'=4,'fsdp'=2,'seq'=4] {'seq'}, dimensions={0}, use_global_device_ids=true | all-gather | bytes 819200 | tf_op jit(solution)/shard_map/all_gather | solution.py:106
  413.1 16.9 %all-gather.19.cloned.1.call-done = bf16[320,4096]{1,0:T(8,128)(2,1)} async-done(((bf16[80,4096]{1,0:T(8,128)(2,1)}), bf16[320,4096]{1,0:T(8,128)(2,1)}) %all-gather.19.cloned.1.call-update) | async-done | bytes 2621456 | tf_op jit(solution)/shard_map/all_gather | solution.py:106
  430.0 4.8 %fusion.124 = (f32[320,2048]{1,0:T(8,128)}, f32[320,2048]{1,0:T(8,128)}) fusion(bf16[320,4096]{1,0:T(8,128)(2,1)} %all-gather.19.cloned.1.call-done), kind=kLoop, calls=%fused_computation.269 | loop fusion | bytes 10485760 | tf_op jit(solution)/shard_map/slice | solution.py:312
  434.7 14.1 %all-gather.17.cloned.1.call-done = bf16[384,1536]{1,0:T(8,128)(2,1)} async-done(((bf16[96,1536]{1,0:T(8,128)(2,1)}), bf16[384,1536]{1,0:T(8,128)(2,1)}) %all-gather.17.cloned.1.call-update) | async-done | bytes 1179664 | tf_op jit(solution)/shard_map/all_gather | solution.py:106
  (273 shorter events, 89.4 us)
Async XLA Ops:
  7.2 6.8 %copy-start.48 = (bf16[320]{0:T(512)(128)(2,1)S(1)}, bf16[320]{0:T(512)(128)(2,1)}, u32[]{:S(2)}) copy-start(bf16[320]{0:T(512)(128)(2,1)} %param.31) | copy-start | bytes 1924
  7.2 6.8 %copy-start.47 = (bf16[320]{0:T(512)(128)(2,1)S(1)}, bf16[320]{0:T(512)(128)(2,1)}, u32[]{:S(2)}) copy-start(bf16[320]{0:T(512)(128)(2,1)} %param.30) | copy-start | bytes 1924
  7.2 6.8 %copy-start.46 = (bf16[320]{0:T(512)(128)(2,1)S(1)}, bf16[320]{0:T(512)(128)(2,1)}, u32[]{:S(2)}) copy-start(bf16[320]{0:T(512)(128)(2,1)} %param.29) | copy-start | bytes 1924
  7.2 6.8 %copy-start.50 = (bf16[128]{0:T(256)(128)(2,1)S(1)}, bf16[128]{0:T(256)(128)(2,1)}, u32[]{:S(2)}) copy-start(bf16[128]{0:T(256)(128)(2,1)} %param.28) | copy-start | bytes 772
  7.2 6.8 %copy-start.49 = (bf16[128]{0:T(256)(128)(2,1)S(1)}, bf16[128]{0:T(256)(128)(2,1)}, u32[]{:S(2)}) copy-start(bf16[128]{0:T(256)(128)(2,1)} %param.27) | copy-start | bytes 772
  7.3 6.8 %copy-start.45 = (bf16[320]{0:T(512)(128)(2,1)S(1)}, bf16[320]{0:T(512)(128)(2,1)}, u32[]{:S(2)}) copy-start(bf16[320]{0:T(512)(128)(2,1)} %param.26) | copy-start | bytes 1924
  7.3 62.6 %all-gather.9.cloned.1.call-start = ((), (), s32[]{:S(2)}) async-start(), calls=%async_computation | async-start | bytes 1310720 | tf_op jit(solution)/shard_map/all_gather | solution.py:204
  10.4 9.5 %collective-permute-start = (bf16[80,1536]{1,0:T(8,128)(2,1)S(1)}, bf16[80,1536]{1,0:T(8,128)(2,1)S(1)}, u32[]{:S(2)}, u32[]{:S(2)}) collective-permute-start(bf16[80,1536]{1,0:T(8,128)(2,1)S(1)} %constant_dynamic-slice_fusion.5), channel_id=1, source_target_pairs={{0,4},{4,0},{1,5},{5,1},{2,6},{6,2},{3,7},{7,3},{8,12},{12,8},{9,1... | collective-permute-start | bytes 737288 | tf_op jit(solution)/shard_map/ppermute | solution.py:68
  31.3 31.3 %copy-start.15 = (f32[256,1536]{1,0:T(8,128)}, f32[256,1536]{1,0:T(8,128)S(1)}, u32[]{:S(2)}) copy-start(f32[256,1536]{1,0:T(8,128)S(1)} %fusion.42) | copy-start | bytes 4718596
  31.3 14.4 %copy-start.30 = (bf16[512,640]{1,0:T(8,128)(2,1)S(1)}, bf16[512,640]{1,0:T(8,128)(2,1)}, u32[]{:S(2)}) copy-start(bf16[512,640]{1,0:T(8,128)(2,1)} %param.22) | copy-start | bytes 1966084
  32.2 37.5 %copy-start.27 = (f32[256,128]{1,0:T(8,128)}, f32[256,128]{1,0:T(8,128)S(1)}, u32[]{:S(2)}) copy-start(f32[256,128]{1,0:T(8,128)S(1)} %get-tuple-element.78) | copy-start | bytes 393220
  32.2 37.5 %copy-start.29 = (f32[256,128]{1,0:T(8,128)}, f32[256,128]{1,0:T(8,128)S(1)}, u32[]{:S(2)}) copy-start(f32[256,128]{1,0:T(8,128)S(1)} %get-tuple-element.79) | copy-start | bytes 393220
  33.0 50.5 %all-gather.13.cloned.1.call-start = ((), (), s32[]{:S(2)}) async-start(), calls=%async_computation.2 | async-start | bytes 1638400 | tf_op jit(solution)/shard_map/all_gather | solution.py:88
  34.8 10.2 %collective-permute-start.3 = (bf16[256,640]{1,0:T(8,128)(2,1)}, bf16[256,640]{1,0:T(8,128)(2,1)S(1)}, u32[]{:S(2)}, u32[]{:S(2)}) collective-permute-start(bf16[256,640]{1,0:T(8,128)(2,1)} %constant_dynamic-slice_fusion.2), channel_id=1, source_target_pairs={{0,4},{4,0},{1,5},{5,1},{2,6},{6,2},{3,7},{7,3},{8,12},{12,8},{9,1... | collective-permute-start | bytes 983048 | tf_op jit(solution)/shard_map/ppermute | solution.py:68
  45.7 51.9 %all-gather.11.cloned.1.call-start = ((), (), s32[]{:S(2)}) async-start(), calls=%async_computation.1 | async-start | bytes 3276800 | tf_op jit(solution)/shard_map/all_gather | solution.py:88
  45.8 8.8 %collective-permute-start.1 = (bf16[128,640]{1,0:T(8,128)(2,1)S(1)}, bf16[128,640]{1,0:T(8,128)(2,1)S(1)}, u32[]{:S(2)}, u32[]{:S(2)}) collective-permute-start(bf16[128,640]{1,0:T(8,128)(2,1)S(1)} %constant_dynamic-slice_fusion.4), channel_id=1, source_target_pairs={{0,4},{4,0},{1,5},{5,1},{2,6},{6,2},{3,7},{7,3},{8,12},{12,8},{9,1... | collective-permute-start | bytes 491528 | tf_op jit(solution)/shard_map/ppermute | solution.py:68
  52.7 16.3 %collective-permute-start.2 = (bf16[80,4096]{1,0:T(8,128)(2,1)}, bf16[80,4096]{1,0:T(8,128)(2,1)}, u32[]{:S(2)}, u32[]{:S(2)}) collective-permute-start(bf16[80,4096]{1,0:T(8,128)(2,1)} %constant_dynamic-slice_fusion.3), channel_id=1, source_target_pairs={{0,4},{4,0},{1,5},{5,1},{2,6},{6,2},{3,7},{7,3},{8,12},{12,8},{9,1... | collective-permute-start | bytes 1966088 | tf_op jit(solution)/shard_map/ppermute | solution.py:68
  69.0 164.9 %all-reduce.10.cloned.1.call-start = ((), (), s32[]{:S(2)}) async-start(), calls=%async_computation.3 | async-start | bytes 655360 | tf_op jit(solution)/shard_map/psum | solution.py:105
  118.9 29.0 %collective-permute-start.9 = (bf16[2,2,80,4096]{3,2,0,1:T(8,128)(2,1)}, bf16[2,2,80,4096]{3,2,0,1:T(8,128)(2,1)}, u32[]{:S(2)}, u32[]{:S(2)}) collective-permute-start(bf16[2,2,80,4096]{3,2,0,1:T(8,128)(2,1)} %bitcast.188), channel_id=1, source_target_pairs={{0,1},{1,0},{2,3},{3,2},{4,5},{5,4},{6,7},{7,6},{8,9},{9,8},{10,11... | collective-permute-start | bytes 7864328 | tf_op jit(solution)/shard_map/ppermute | solution.py:68
  125.8 115.8 %collective-permute-start.6 = (bf16[2,2,128,640]{3,2,1,0:T(8,128)(2,1)}, bf16[2,2,128,640]{3,2,1,0:T(8,128)(2,1)}, u32[]{:S(2)}, u32[]{:S(2)}) collective-permute-start(bf16[2,2,128,640]{3,2,1,0:T(8,128)(2,1)} %dynamic-slice_bitcast_fusion.4), channel_id=1, source_target_pairs={{0,1},{1,0},{2,3},{3,2},{4,5},{5,4},{6,7},{7,6},{8,9},{9,8},{10,11... | collective-permute-start | bytes 1966088 | tf_op jit(solution)/shard_map/ppermute | solution.py:68
  129.8 22.6 %collective-permute-start.12 = (bf16[2,2,256,640]{3,2,1,0:T(8,128)(2,1)}, bf16[2,2,256,640]{3,2,1,0:T(8,128)(2,1)}, u32[]{:S(2)}, u32[]{:S(2)}) collective-permute-start(bf16[2,2,256,640]{3,2,1,0:T(8,128)(2,1)} %dynamic-slice_bitcast_fusion), channel_id=1, source_target_pairs={{0,1},{1,0},{2,3},{3,2},{4,5},{5,4},{6,7},{7,6},{8,9},{9,8},{10,11... | collective-permute-start | bytes 3932168 | tf_op jit(solution)/shard_map/ppermute | solution.py:68
  152.0 31.3 %collective-permute-start.10 = (bf16[2,80,4096]{2,1,0:T(8,128)(2,1)}, bf16[2,80,4096]{2,1,0:T(8,128)(2,1)}, u32[]{:S(2)}, u32[]{:S(2)}) collective-permute-start(bf16[2,80,4096]{2,1,0:T(8,128)(2,1)} %dynamic-slice_bitcast_fusion.1), channel_id=1, source_target_pairs={{0,2},{1,3},{2,0},{3,1},{4,6},{5,7},{6,4},{7,5},{8,10},{9,11},{10,... | collective-permute-start | bytes 3932168 | tf_op jit(solution)/shard_map/ppermute | solution.py:68
  156.9 18.6 %collective-permute-start.13 = (bf16[2,256,640]{2,1,0:T(8,128)(2,1)}, bf16[2,256,640]{2,1,0:T(8,128)(2,1)}, u32[]{:S(2)}, u32[]{:S(2)}) collective-permute-start(bf16[2,256,640]{2,1,0:T(8,128)(2,1)} %dynamic-slice_bitcast_fusion.2), channel_id=1, source_target_pairs={{0,4},{4,0},{1,5},{5,1},{2,6},{6,2},{3,7},{7,3},{8,12},{12,8},{9,1... | collective-permute-start | bytes 1966088 | tf_op jit(solution)/shard_map/ppermute | solution.py:68
  161.7 12.3 %copy-start.28 = (f32[256,128]{1,0:T(8,128)S(1)}, f32[256,128]{1,0:T(8,128)}, u32[]{:S(2)}) copy-start(f32[256,128]{1,0:T(8,128)} %copy-done.27) | copy-start | bytes 393220
  174.0 9.3 %copy-start.2 = (bf16[2,2,80,4096]{3,2,0,1:T(8,128)(2,1)S(1)}, bf16[2,2,80,4096]{3,2,0,1:T(8,128)(2,1)}, u32[]{:S(2)}) copy-start(bf16[2,2,80,4096]{3,2,0,1:T(8,128)(2,1)} %copy-done.1) | copy-start | bytes 7864324
  175.5 14.4 %copy-start.10 = (f32[256,4,128]{2,0,1:T(8,128)}, f32[256,4,128]{2,0,1:T(8,128)S(1)}, u32[]{:S(2)}) copy-start(f32[256,4,128]{2,0,1:T(8,128)S(1)} %get-tuple-element.58) | copy-start | bytes 1572868
  175.5 14.4 %copy-start.11 = (f32[256,4,128]{2,0,1:T(8,128)}, f32[256,4,128]{2,0,1:T(8,128)S(1)}, u32[]{:S(2)}) copy-start(f32[256,4,128]{2,0,1:T(8,128)S(1)} %get-tuple-element.59) | copy-start | bytes 1572868
  177.4 11.7 %copy-start.12 = (bf16[1024,512]{1,0:T(8,128)(2,1)S(1)}, bf16[1024,512]{1,0:T(8,128)(2,1)}, u32[]{:S(2)}) copy-start(bf16[1024,512]{1,0:T(8,128)(2,1)} %copy.140) | copy-start | bytes 3145732
  187.0 16.4 %collective-permute-start.11 = (bf16[80,4096]{1,0:T(8,128)(2,1)}, bf16[80,4096]{1,0:T(8,128)(2,1)}, u32[]{:S(2)}, u32[]{:S(2)}) collective-permute-start(bf16[80,4096]{1,0:T(8,128)(2,1)} %dynamic-slice_bitcast_fusion.3), channel_id=1, source_target_pairs={{0,4},{4,0},{1,5},{5,1},{2,6},{6,2},{3,7},{7,3},{8,12},{12,8},{9,1... | collective-permute-start | bytes 1966088 | tf_op jit(solution)/shard_map/ppermute | solution.py:68
  188.5 8.8 %collective-permute-start.14 = (bf16[256,640]{1,0:T(8,128)(2,1)S(1)}, bf16[256,640]{1,0:T(8,128)(2,1)S(1)}, u32[]{:S(2)}, u32[]{:S(2)}) collective-permute-start(bf16[256,640]{1,0:T(8,128)(2,1)S(1)} %dynamic-slice_bitcast_fusion.7), channel_id=1, source_target_pairs={{0,2},{1,3},{2,0},{3,1},{4,6},{5,7},{6,4},{7,5},{8,10},{9,11},{10,... | collective-permute-start | bytes 983048 | tf_op jit(solution)/shard_map/ppermute | solution.py:68
  189.9 48.6 %collective-permute-start.4 = (bf16[2,256,512]{2,1,0:T(8,128)(2,1)}, bf16[2,256,512]{2,1,0:T(8,128)(2,1)}, u32[]{:S(2)}, u32[]{:S(2)}) collective-permute-start(bf16[2,256,512]{2,1,0:T(8,128)(2,1)} %dynamic-slice_bitcast_fusion.6), channel_id=1, source_target_pairs={{0,1},{1,0},{2,3},{3,2},{4,5},{5,4},{6,7},{7,6},{8,9},{9,8},{10,11... | collective-permute-start | bytes 1572872 | tf_op jit(solution)/shard_map/ppermute | solution.py:68
  198.1 78.8 %all-reduce.12.cloned.1.call-start = ((), (), s32[]{:S(2)}) async-start(), calls=%async_computation.4 | async-start | bytes 1310720 | tf_op jit(solution)/shard_map/psum | solution.py:105
  233.9 62.3 %all-gather.15.cloned.1.call-start = ((), (), s32[]{:S(2)}) async-start(), calls=%async_computation.6 | async-start | bytes 1638400 | tf_op jit(solution)/shard_map/all_gather | solution.py:106
  239.9 6.4 %collective-permute-start.5 = (bf16[256,512]{1,0:T(8,128)(2,1)S(1)}, bf16[256,512]{1,0:T(8,128)(2,1)S(1)}, u32[]{:S(2)}, u32[]{:S(2)}) collective-permute-start(bf16[256,512]{1,0:T(8,128)(2,1)S(1)} %dynamic-slice_bitcast_fusion.10), channel_id=1, source_target_pairs={{0,2},{1,3},{2,0},{3,1},{4,6},{5,7},{6,4},{7,5},{8,10},{9,11},{10,... | collective-permute-start | bytes 786440 | tf_op jit(solution)/shard_map/ppermute | solution.py:68
  241.5 92.4 %all-reduce.14.cloned.1.call-start = ((), (), s32[]{:S(2)}) async-start(), calls=%async_computation.5 | async-start | bytes 327680 | tf_op jit(solution)/shard_map/psum | solution.py:105
  242.9 7.3 %collective-permute-start.7 = (bf16[2,128,640]{2,1,0:T(8,128)(2,1)S(1)}, bf16[2,128,640]{2,1,0:T(8,128)(2,1)S(1)}, u32[]{:S(2)}, u32[]{:S(2)}) collective-permute-start(bf16[2,128,640]{2,1,0:T(8,128)(2,1)S(1)} %dynamic-slice_bitcast_fusion.8), channel_id=1, source_target_pairs={{0,4},{4,0},{1,5},{5,1},{2,6},{6,2},{3,7},{7,3},{8,12},{12,8},{9,1... | collective-permute-start | bytes 983048 | tf_op jit(solution)/shard_map/ppermute | solution.py:68
  246.5 30.6 %copy-start.18 = (bf16[256,4,256]{0,2,1:T(8,128)(2,1)S(1)}, bf16[256,4,256]{0,2,1:T(8,128)(2,1)}, u32[]{:S(2)}) copy-start(bf16[256,4,256]{0,2,1:T(8,128)(2,1)} %copy.138) | copy-start | bytes 1572868
  250.3 5.4 %collective-permute-start.8 = (bf16[128,640]{1,0:T(8,128)(2,1)S(1)}, bf16[128,640]{1,0:T(8,128)(2,1)S(1)}, u32[]{:S(2)}, u32[]{:S(2)}) collective-permute-start(bf16[128,640]{1,0:T(8,128)(2,1)S(1)} %dynamic-slice_bitcast_fusion.11), channel_id=1, source_target_pairs={{0,2},{1,3},{2,0},{3,1},{4,6},{5,7},{6,4},{7,5},{8,10},{9,11},{10,... | collective-permute-start | bytes 491528 | tf_op jit(solution)/shard_map/ppermute | solution.py:68
  277.0 126.1 %all-reduce.16.cloned.1.call-start = ((), (), s32[]{:S(2)}) async-start(), calls=%async_computation.7 | async-start | bytes 589824 | tf_op jit(solution)/shard_map/psum | solution.py:105
  277.0 56.8 %copy-start.32 = (bf16[320,1536]{1,0:T(8,128)(2,1)S(1)}, bf16[320,1536]{1,0:T(8,128)(2,1)}, u32[]{:S(2)}) copy-start(bf16[320,1536]{1,0:T(8,128)(2,1)} %copy-done.31) | copy-start | bytes 2949124
  278.1 55.8 %copy-start.16 = (bf16[256,1536]{0,1:T(8,128)(2,1)}, bf16[256,1536]{0,1:T(8,128)(2,1)S(1)}, u32[]{:S(2)}) copy-start(bf16[256,1536]{0,1:T(8,128)(2,1)S(1)} %pad_maximum_fusion.16) | copy-start | bytes 2359300
  339.3 2.9 collective-permute-start.15
  342.6 60.5 %copy-start.44 = (bf16[128,640]{1,0:T(8,128)(2,1)S(1)}, bf16[128,640]{1,0:T(8,128)(2,1)}, u32[]{:S(2)}) copy-start(bf16[128,640]{1,0:T(8,128)(2,1)} %all-reduce.14.cloned.1.call-done) | copy-start | bytes 491524
  342.6 15.4 %collective-permute-start.16 = (bf16[2,96,1536]{2,1,0:T(8,128)(2,1)S(1)}, bf16[2,96,1536]{2,1,0:T(8,128)(2,1)S(1)}, u32[]{:S(2)}, u32[]{:S(2)}) collective-permute-start(bf16[2,96,1536]{2,1,0:T(8,128)(2,1)S(1)} %dynamic-slice_bitcast_fusion.5), channel_id=1, source_target_pairs={{0,4},{4,0},{1,5},{5,1},{2,6},{6,2},{3,7},{7,3},{8,12},{12,8},{9,1... | collective-permute-start | bytes 1769480 | tf_op jit(solution)/shard_map/ppermute | solution.py:68
  358.2 53.9 %copy-start.34 = (f32[256,640]{1,0:T(8,128)S(1)}, f32[256,640]{1,0:T(8,128)}, u32[]{:S(2)}) copy-start(f32[256,640]{1,0:T(8,128)} %get-tuple-element.89) | copy-start | bytes 1966084
  358.2 8.3 %collective-permute-start.17 = (bf16[96,1536]{1,0:T(8,128)(2,1)S(1)}, bf16[96,1536]{1,0:T(8,128)(2,1)S(1)}, u32[]{:S(2)}, u32[]{:S(2)}) collective-permute-start(bf16[96,1536]{1,0:T(8,128)(2,1)S(1)} %dynamic-slice_bitcast_fusion.9), channel_id=1, source_target_pairs={{0,2},{1,3},{2,0},{3,1},{4,6},{5,7},{6,4},{7,5},{8,10},{9,11},{10,... | collective-permute-start | bytes 884744 | tf_op jit(solution)/shard_map/ppermute | solution.py:68
  367.3 62.7 %all-gather.19.cloned.1.call-start = ((), (), s32[]{:S(2)}) async-start(), calls=%async_computation.9 | async-start | bytes 3276800 | tf_op jit(solution)/shard_map/all_gather | solution.py:106
  368.0 80.8 %all-gather.17.cloned.1.call-start = ((), (), s32[]{:S(2)}) async-start(), calls=%async_computation.8 | async-start | bytes 1474560 | tf_op jit(solution)/shard_map/all_gather | solution.py:106
  (32 other events, 80.5 us)
Sparse Core Ops, SparseCore 0:
  33.1 16.9 all-gather.8
  52.3 18.1 all-gather.12
  72.0 25.5 all-gather.10
  198.3 35.5 all-reduce.9
  236.6 40.3 all-reduce.11
  278.4 17.6 all-gather.14
  299.0 34.8 all-reduce.13
  367.4 35.6 all-reduce.15
  404.7 25.2 all-gather.18
  431.4 17.4 all-gather.16
where the time goes:
time: 470 us; the launch traced here: 462 us
  waiting for transfers between devices  242 us (51%)
  matrix products  57.4 us (12%)
  local copies, waits for them, and re-layouts  50.7 us (11%)
  other arithmetic  47.7 us (10%)
  blocking collectives  30.1 us (6%)
  starting transfers between devices  18.4 us (4%)
  between operations  15.4 us (3%)
    psum x4, waiting for transfers between devices, reduce_blocks(): part = lax.psum(part, 'rep')  118 us
    ppermute x18, waiting for transfers between devices, swap(): return lax.ppermute(values, axis_name, [(i, i ^ bit) for i in range(size)])  62.7 us
    all_gather x3, waiting for transfers between devices, reduce_blocks(): lax.all_gather(part, 'seq', axis=0, tiled=True).reshape(4, rows, columns)  49 us
    dot_general x6, matrix products, transpose_times(): lax.dot_general(left_side, right_side, (((0,), (0,)), ((), ())), preferre...  21.6 us
    dot_general x6, matrix products, matmul(): return jnp.dot(left_side, right_side, preferred_element_type=jnp.float32)  20.7 us
    ppermute x18, starting transfers between devices, swap(): return lax.ppermute(values, axis_name, [(i, i ^ bit) for i in range(size)])  18 us
    all_gather x2, blocking collectives, gather_rows(): other = lax.all_gather(swap(piece, 'fsdp', 1), 'seq', axis=0, tiled=True)  16.8 us
    convert_element_type x13, other arithmetic, halve(): (kept.astype(jnp.float32) + arrived.astype(jnp.float32)).astype(jnp.bfloa...  15.8 us
  transfers between devices with their start and end apart: 28, of which 19 were waited for; matrix products, arithmetic and copies ran while one was open for 23% of the time, Pallas kernels for 0%

commit v1 on v0

--- a/solution.py
+++ b/solution.py
@@ -102,7 +102,7 @@
         part = halve(part, "fsdp", 1, 0)
     if before is not None:
         part, _ = lax.optimization_barrier((part, before))
-    part = lax.psum(part, "rep")
+    part = jnp.sum(lax.all_gather(part, "rep"), axis=0)
     return (lax.all_gather(part, "seq", axis=0, tiled=True).reshape(4, rows, columns), part)
 
 

time: 470 us -> 426 us (0.906)
  waiting for transfers between devices: 242 us -> 168 us
  blocking collectives: 30.1 us -> 47.3 us
  other arithmetic: 47.7 us -> 56.5 us
  matrix products: 57.4 us -> 62.8 us
    psum x4 -> x0, waiting for transfers between devices: 118 us -> none  [reduce_blocks(): part = lax.psum(part, 'rep')]
    all_gather x0 -> x3, waiting for transfers between devices: none -> 38.7 us  [reduce_blocks(): part = jnp.sum(lax.all_gather(part, 'rep'), axis=0)]
    ppermute x18, waiting for transfers between devices: 62.7 us -> 93.9 us  [swap(): return lax.ppermute(values, axis_name, [(i, i ^ bit) for i in range(size)])]
    all_gather x3, waiting for transfers between devices: 49 us -> 29.5 us  [reduce_blocks(): lax.all_gather(part, 'seq', axis=0, tiled=True).reshape(4, rows, columns)]
    all_gather x0 -> x1, blocking collectives: none -> 17.1 us  [reduce_blocks(): part = jnp.sum(lax.all_gather(part, 'rep'), axis=0)]
    reduce_sum x0 -> x4, other arithmetic: none -> 8.56 us  [reduce_blocks(): part = jnp.sum(lax.all_gather(part, 'rep'), axis=0)]
    all_gather x2, waiting for transfers between devices: 10.7 us -> 5.33 us  [gather_rows(): other = lax.all_gather(swap(piece, 'fsdp', 1), 'seq', axis=0, tiled=True)]
    squeeze x12 -> x13, local copies, waits for them, and re-layouts: 6.2 us -> 10.4 us  [halve(): sent = lax.dynamic_index_in_dim(values, 1 - mine, dim, keepdims=False)]
  transfers between devices with their start and end apart: 28 -> 27, of which waited for: 19 -> 17; matrix products, arithmetic and copies ran while one was open for 23% -> 29% of each run, Pallas kernels for 0% -> 0%
where the time goes in v1:
time: 426 us; the launch traced here: 418 us
  waiting for transfers between devices  168 us (39%)
  matrix products  62.8 us (15%)
  other arithmetic  56.5 us (13%)
  local copies, waits for them, and re-layouts  49.3 us (12%)
  blocking collectives  47.3 us (11%)
  starting transfers between devices  18.3 us (4%)
  between operations  15.2 us (4%)
    ppermute x18, waiting for transfers between devices, swap(): return lax.ppermute(values, axis_name, [(i, i ^ bit) for i in range(size)])  93.9 us
    all_gather x3, waiting for transfers between devices, reduce_blocks(): part = jnp.sum(lax.all_gather(part, 'rep'), axis=0)  38.7 us
    all_gather x3, waiting for transfers between devices, reduce_blocks(): lax.all_gather(part, 'seq', axis=0, tiled=True).reshape(4, rows, columns)  29.5 us
    dot_general x6, matrix products, transpose_times(): lax.dot_general(left_side, right_side, (((0,), (0,)), ((), ())), preferre...  21.9 us
    dot_general x6, matrix products, matmul(): return jnp.dot(left_side, right_side, preferred_element_type=jnp.float32)  21.1 us
    dot_general x6, matrix products, times_transpose(): lax.dot_general(left_side, right_side, (((1,), (1,)), ((), ())), preferre...  19.7 us
    ppermute x18, starting transfers between devices, swap(): return lax.ppermute(values, axis_name, [(i, i ^ bit) for i in range(size)])  17.7 us
    all_gather x1, blocking collectives, reduce_blocks(): part = jnp.sum(lax.all_gather(part, 'rep'), axis=0)  17.1 us
  transfers between devices with their start and end apart: 27, of which 17 were waited for; matrix products, arithmetic and copies ran while one was open for 29% of the time, Pallas kernels for 0%

profile of v1, /device:TPU:0, one launch (start us, length us, event | category | flops | bytes accessed | tf_op | source)
XLA Modules:
  0.0 417.8 jit_solution(5455220448694508002)
XLA Ops:
  10.4 3.0 collective-permute-start
  14.1 5.5 %all-gather.5 = bf16[2,1,1536]{2,1,0:T(2,128)(2,1)S(1)} all-gather(bf16[1,1,1536]{2,1,0:T(2,128)(2,1)S(1)} %reshape.534), channel_id=2, replica_groups=mesh['rep'=4,'fsdp'=2,'seq'=4] {'fsdp'}, dimensions={0}, use_global_device_ids=true | all-gather | bytes 9216 | tf_op jit(solution)/shard_map/all_gather | solution.py:160
  20.0 9.9 %all_gather.55 = bf16[320,1536]{1,0:T(8,128)(2,1)S(1)} all-gather(bf16[80,1536]{1,0:T(8,128)(2,1)S(1)} %collective-permute-done), channel_id=1, replica_groups=mesh['rep'=4,'fsdp'=2,'seq'=4] {'seq'}, dimensions={0}, use_global_device_ids=true | all-gather | bytes 1228800 | tf_op jit(solution)/shard_map/all_gather | solution.py:88
  35.6 8.5 %collective-permute-done.3 = bf16[256,640]{1,0:T(8,128)(2,1)S(1)} collective-permute-done((bf16[256,640]{1,0:T(8,128)(2,1)S(1)}, bf16[256,640]{1,0:T(8,128)(2,1)S(1)}, u32[]{:S(2)}, u32[]{:S(2)}) %collective-permute-start.3) | collective-permute-done | bytes 327712 | tf_op jit(solution)/shard_map/ppermute | solution.py:68
  54.6 15.4 %collective-permute-done.1 = bf16[128,640]{1,0:T(8,128)(2,1)S(1)} collective-permute-done((bf16[128,640]{1,0:T(8,128)(2,1)S(1)}, bf16[128,640]{1,0:T(8,128)(2,1)S(1)}, u32[]{:S(2)}, u32[]{:S(2)}) %collective-permute-start.1) | collective-permute-done | bytes 163872 | tf_op jit(solution)/shard_map/ppermute | solution.py:68
  70.1 6.8 %all_gather.57 = bf16[512,640]{1,0:T(8,128)(2,1)S(1)} all-gather(bf16[128,640]{1,0:T(8,128)(2,1)S(1)} %collective-permute-done.1), channel_id=1, replica_groups=mesh['rep'=4,'fsdp'=2,'seq'=4] {'seq'}, dimensions={0}, use_global_device_ids=true | all-gather | bytes 819200 | tf_op jit(solution)/shard_map/all_gather | solution.py:88
  77.0 2.3 broadcast_select_fusion.7
  81.2 2.0 fusion.126
  87.6 2.6 reshape.502
  90.2 2.5 convolution_convert_fusion.6
  95.3 3.4 broadcast_select_fusion.3
  98.7 5.3 %all-gather.18.cloned.1.call-done = bf16[320,4096]{1,0:T(8,128)(2,1)} async-done(((bf16[80,4096]{1,0:T(8,128)(2,1)}), bf16[320,4096]{1,0:T(8,128)(2,1)}) %all-gather.18.cloned.1.call-update) | async-done | bytes 2621456 | tf_op jit(solution)/shard_map/all_gather | solution.py:88
  104.0 2.9 broadcast_select_fusion.1
  113.4 4.6 %fusion.23 = (bf16[256,2048]{1,0:T(8,128)(2,1)S(1)}, bf16[256,2048]{1,0:T(8,128)(2,1)S(1)}) fusion(f32[256,4096]{1,0:T(8,128)S(1)} %fusion.5, bf16[256,640]{1,0:T(8,128)(2,1)S(1)} %get-tuple-element.62, bf16[1024,640]{1,0:T(8,128)(2,1)S(1)} %copy-done.22, bf16[1024,640]{1,0:T(8,128)(2,1)S(1)} %copy-done.21), kind=kOutput, calls=%fused_computation.41 | convolution fusion | flops 688914432 | bytes 9240576 | tf_op jit(solution)/shard_map/dot_general | solution.py:51
  122.6 2.0 dynamic-slice_bitcast_fusion
  126.0 5.2 %multiply_reduce_fusion.3 = (bf16[640]{0:T(1024)(128)(2,1)S(1)}, f32[256]{0:T(256)S(1)}, f32[256,640]{1,0:T(8,128)S(1)}) fusion(f32[256,640]{1,0:T(8,128)S(1)} %get-tuple-element.43, f32[256]{0:T(256)S(1)} %fusion.102, f32[640]{0:T(1024)S(1)} %reshape.511, bf16[320,4096]{1,0:T(8,128)(2,1)} %copy-done.16, bf16[320,4096]{1,0:T(8,128)(2,1)} %copy-done.15, ...), kind=kOutput, calls=%fused_computation.128 | convolution fusion | flops 1357839488 | bytes 8656640 | tf_op jit(solution)/shard_map/dot_general | solution.py:51
  135.0 15.0 %collective-permute-done.13 = bf16[2,256,640]{2,1,0:T(8,128)(2,1)S(1)} collective-permute-done((bf16[2,256,640]{2,1,0:T(8,128)(2,1)S(1)}, bf16[2,256,640]{2,1,0:T(8,128)(2,1)S(1)}, u32[]{:S(2)}, u32[]{:S(2)}) %collective-permute-start.13) | collective-permute-done | bytes 655392 | tf_op jit(solution)/shard_map/ppermute | solution.py:68
  150.6 2.7 fusion.1
  157.3 3.6 collective-permute-done.14
  161.8 2.0 convolution_convert_fusion.5
  168.5 2.7 fusion.71
  171.2 16.3 %collective-permute-done.10 = bf16[2,80,4096]{2,1,0:T(8,128)(2,1)} collective-permute-done((bf16[2,80,4096]{2,1,0:T(8,128)(2,1)}, bf16[2,80,4096]{2,1,0:T(8,128)(2,1)}, u32[]{:S(2)}, u32[]{:S(2)}) %collective-permute-start.10) | collective-permute-done | bytes 1310752 | tf_op jit(solution)/shard_map/ppermute | solution.py:68
  187.5 2.8 fusion.9
  190.3 4.1 all-gather.28.cloned.1.call-done
  194.4 2.3 reduce_sum.309
  200.4 12.9 %fusion.38 = bf16[1024,256]{0,1:T(8,128)(2,1)} fusion(f32[256,4,1024]{2,0,1:T(8,128)} %fusion.71, f32[256,4,1024]{2,0,1:T(8,128)} %copy-done.2, f32[256,4]{0,1:T(4,128)S(1)} %log_add_fusion, bf16[256,4,128]{2,0,1:T(8,128)(2,1)} %copy-done.37, bf16[256,4,128]{2,0,1:T(8,128)(2,1)} %copy-done.36), kind=kOutput, calls=%fused_computation.72 | convolution fusion | flops 545523712 | bytes 9441280 | tf_op jit(solution)/shard_map/dot_general | solution.py:57
  213.4 2.5 convolution_convert_fusion.4
  216.9 2.3 copy.120
  219.2 2.3 fusion.36
  223.4 13.0 %fusion.15 = f32[256,4,256]{2,0,1:T(8,128)} fusion(f32[256,4,1024]{2,0,1:T(8,128)} %fusion.71, f32[256,4,1024]{2,0,1:T(8,128)} %copy-done.2, f32[256,4]{0,1:T(4,128)S(1)} %log_add_fusion, bf16[1024,512]{1,0:T(8,128)(2,1)} %all-gather.16.cloned.1.call-done), kind=kOutput, calls=%fused_computation.32 | convolution fusion | flops 544212992 | bytes 18358272 | tf_op jit(solution)/shard_map/dot_general | solution.py:47
  239.3 2.4 fusion.48
  241.6 2.0 copy.118
  248.9 4.8 %collective-permute-done.5 = bf16[256,512]{1,0:T(8,128)(2,1)S(1)} collective-permute-done((bf16[256,512]{1,0:T(8,128)(2,1)S(1)}, bf16[256,512]{1,0:T(8,128)(2,1)S(1)}, u32[]{:S(2)}, u32[]{:S(2)}) %collective-permute-start.5) | collective-permute-done | bytes 262176 | tf_op jit(solution)/shard_map/ppermute | solution.py:68
  260.5 4.8 %collective-permute-done.8 = bf16[128,640]{1,0:T(8,128)(2,1)S(1)} collective-permute-done((bf16[128,640]{1,0:T(8,128)(2,1)S(1)}, bf16[128,640]{1,0:T(8,128)(2,1)S(1)}, u32[]{:S(2)}, u32[]{:S(2)}) %collective-permute-start.8) | collective-permute-done | bytes 163872 | tf_op jit(solution)/shard_map/ppermute | solution.py:68
  265.4 3.0 convert_element_type.445
  268.3 6.2 %all-gather.30.cloned.1.call-done = bf16[320,4096]{1,0:T(8,128)(2,1)} async-done(((bf16[80,4096]{1,0:T(8,128)(2,1)}), bf16[320,4096]{1,0:T(8,128)(2,1)}) %all-gather.30.cloned.1.call-update) | async-done | bytes 2621456 | tf_op jit(solution)/shard_map/all_gather | solution.py:105
  274.6 3.2 reduce_sum.310
  277.8 17.1 %all-gather.3 = bf16[512,640]{1,0:T(8,128)(2,1)S(1)} all-gather(bf16[128,640]{1,0:T(8,128)(2,1)S(1)} %fusion.80), channel_id=5, replica_groups=mesh['rep'=4,'fsdp'=2,'seq'=4] {'rep'}, dimensions={0}, use_global_device_ids=true | all-gather | bytes 819200 | tf_op jit(solution)/shard_map/all_gather | solution.py:105
  295.7 3.2 fusion.59
  301.5 2.8 collective-permute-done.15
  306.1 14.0 %collective-permute-done.16 = bf16[2,96,1536]{2,1,0:T(8,128)(2,1)S(1)} collective-permute-done((bf16[2,96,1536]{2,1,0:T(8,128)(2,1)S(1)}, bf16[2,96,1536]{2,1,0:T(8,128)(2,1)S(1)}, u32[]{:S(2)}, u32[]{:S(2)}) %collective-permute-start.16) | collective-permute-done | bytes 589856 | tf_op jit(solution)/shard_map/ppermute | solution.py:68
  321.8 6.8 %collective-permute-done.17 = bf16[96,1536]{1,0:T(8,128)(2,1)S(1)} collective-permute-done((bf16[96,1536]{1,0:T(8,128)(2,1)S(1)}, bf16[96,1536]{1,0:T(8,128)(2,1)S(1)}, u32[]{:S(2)}, u32[]{:S(2)}) %collective-permute-start.17) | collective-permute-done | bytes 294944 | tf_op jit(solution)/shard_map/ppermute | solution.py:68
  330.2 28.4 %all-gather.32.cloned.1.call-done = bf16[384,1536]{1,0:T(8,128)(2,1)} async-done(((bf16[96,1536]{1,0:T(8,128)(2,1)}), bf16[384,1536]{1,0:T(8,128)(2,1)}) %all-gather.32.cloned.1.call-update) | async-done | bytes 1179664 | tf_op jit(solution)/shard_map/all_gather | solution.py:105
  358.6 2.3 reduce_sum.319
  361.0 7.9 %all_gather.70 = bf16[512,640]{1,0:T(8,128)(2,1)S(1)} all-gather(bf16[128,640]{1,0:T(8,128)(2,1)S(1)} %copy-done.32), channel_id=1, replica_groups=mesh['rep'=4,'fsdp'=2,'seq'=4] {'seq'}, dimensions={0}, use_global_device_ids=true | all-gather | bytes 819200 | tf_op jit(solution)/shard_map/all_gather | solution.py:106
  371.0 14.6 %all-gather.26.cloned.1.call-done = bf16[320,4096]{1,0:T(8,128)(2,1)} async-done(((bf16[80,4096]{1,0:T(8,128)(2,1)}), bf16[320,4096]{1,0:T(8,128)(2,1)}) %all-gather.26.cloned.1.call-update) | async-done | bytes 2621456 | tf_op jit(solution)/shard_map/all_gather | solution.py:106
  385.6 4.8 %fusion.124 = (f32[320,2048]{1,0:T(8,128)}, f32[320,2048]{1,0:T(8,128)}) fusion(bf16[320,4096]{1,0:T(8,128)(2,1)} %all-gather.26.cloned.1.call-done), kind=kLoop, calls=%fused_computation.266 | loop fusion | bytes 10485760 | tf_op jit(solution)/shard_map/slice | solution.py:312
  390.3 14.9 %all-gather.24.cloned.1.call-done = bf16[384,1536]{1,0:T(8,128)(2,1)} async-done(((bf16[96,1536]{1,0:T(8,128)(2,1)}), bf16[384,1536]{1,0:T(8,128)(2,1)}) %all-gather.24.cloned.1.call-update) | async-done | bytes 1179664 | tf_op jit(solution)/shard_map/all_gather | solution.py:106
  (262 shorter events, 92.8 us)
Async XLA Ops:
  7.2 6.3 %copy-start.45 = (s32[1,3]{1,0:T(1,128)S(1)}, s32[1,3]{1,0:T(1,128)}, u32[]{:S(2)}) copy-start(s32[1,3]{1,0:T(1,128)} %param.18) | copy-start | bytes 40
  7.2 6.5 %copy-start.8 = (bf16[1,256,640]{2,1,0:T(8,128)(2,1)S(1)}, bf16[1,256,640]{2,1,0:T(8,128)(2,1)}, u32[]{:S(2)}) copy-start(bf16[1,256,640]{2,1,0:T(8,128)(2,1)} %param.16) | copy-start | bytes 983044
  7.2 6.8 %copy-start.42 = (bf16[320]{0:T(512)(128)(2,1)S(1)}, bf16[320]{0:T(512)(128)(2,1)}, u32[]{:S(2)}) copy-start(bf16[320]{0:T(512)(128)(2,1)} %param.31) | copy-start | bytes 1924
  7.2 6.8 %copy-start.41 = (bf16[320]{0:T(512)(128)(2,1)S(1)}, bf16[320]{0:T(512)(128)(2,1)}, u32[]{:S(2)}) copy-start(bf16[320]{0:T(512)(128)(2,1)} %param.30) | copy-start | bytes 1924
  7.2 6.8 %copy-start.40 = (bf16[320]{0:T(512)(128)(2,1)S(1)}, bf16[320]{0:T(512)(128)(2,1)}, u32[]{:S(2)}) copy-start(bf16[320]{0:T(512)(128)(2,1)} %param.29) | copy-start | bytes 1924
  7.2 6.8 %copy-start.44 = (bf16[128]{0:T(256)(128)(2,1)S(1)}, bf16[128]{0:T(256)(128)(2,1)}, u32[]{:S(2)}) copy-start(bf16[128]{0:T(256)(128)(2,1)} %param.28) | copy-start | bytes 772
  7.2 6.8 %copy-start.43 = (bf16[128]{0:T(256)(128)(2,1)S(1)}, bf16[128]{0:T(256)(128)(2,1)}, u32[]{:S(2)}) copy-start(bf16[128]{0:T(256)(128)(2,1)} %param.27) | copy-start | bytes 772
  7.3 6.8 %copy-start.39 = (bf16[320]{0:T(512)(128)(2,1)S(1)}, bf16[320]{0:T(512)(128)(2,1)}, u32[]{:S(2)}) copy-start(bf16[320]{0:T(512)(128)(2,1)} %param.26) | copy-start | bytes 1924
  7.3 73.5 %all-gather.16.cloned.1.call-start = ((), (), s32[]{:S(2)}) async-start(), calls=%async_computation | async-start | bytes 1310720 | tf_op jit(solution)/shard_map/all_gather | solution.py:204
  10.4 9.5 %collective-permute-start = (bf16[80,1536]{1,0:T(8,128)(2,1)S(1)}, bf16[80,1536]{1,0:T(8,128)(2,1)S(1)}, u32[]{:S(2)}, u32[]{:S(2)}) collective-permute-start(bf16[80,1536]{1,0:T(8,128)(2,1)S(1)} %constant_dynamic-slice_fusion.3), channel_id=1, source_target_pairs={{0,4},{4,0},{1,5},{5,1},{2,6},{6,2},{3,7},{7,3},{8,12},{12,8},{9,1... | collective-permute-start | bytes 737288 | tf_op jit(solution)/shard_map/ppermute | solution.py:68
  31.3 48.0 %copy-start.11 = (f32[256,1536]{1,0:T(8,128)}, f32[256,1536]{1,0:T(8,128)S(1)}, u32[]{:S(2)}) copy-start(f32[256,1536]{1,0:T(8,128)S(1)} %fusion.42) | copy-start | bytes 4718596
  32.2 48.4 %copy-start.23 = (f32[256,128]{1,0:T(8,128)}, f32[256,128]{1,0:T(8,128)S(1)}, u32[]{:S(2)}) copy-start(f32[256,128]{1,0:T(8,128)S(1)} %get-tuple-element.76) | copy-start | bytes 393220
  32.2 48.4 %copy-start.25 = (f32[256,128]{1,0:T(8,128)}, f32[256,128]{1,0:T(8,128)S(1)}, u32[]{:S(2)}) copy-start(f32[256,128]{1,0:T(8,128)S(1)} %get-tuple-element.77) | copy-start | bytes 393220
  33.0 62.3 %all-gather.20.cloned.1.call-start = ((), (), s32[]{:S(2)}) async-start(), calls=%async_computation.2 | async-start | bytes 1638400 | tf_op jit(solution)/shard_map/all_gather | solution.py:88
  34.1 10.0 %collective-permute-start.3 = (bf16[256,640]{1,0:T(8,128)(2,1)S(1)}, bf16[256,640]{1,0:T(8,128)(2,1)S(1)}, u32[]{:S(2)}, u32[]{:S(2)}) collective-permute-start(bf16[256,640]{1,0:T(8,128)(2,1)S(1)} %constant_dynamic-slice_fusion), channel_id=1, source_target_pairs={{0,4},{4,0},{1,5},{5,1},{2,6},{6,2},{3,7},{7,3},{8,12},{12,8},{9,1... | collective-permute-start | bytes 983048 | tf_op jit(solution)/shard_map/ppermute | solution.py:68
  44.8 59.2 %all-gather.18.cloned.1.call-start = ((), (), s32[]{:S(2)}) async-start(), calls=%async_computation.1 | async-start | bytes 3276800 | tf_op jit(solution)/shard_map/all_gather | solution.py:88
  50.2 26.7 %collective-permute-start.2 = (bf16[80,4096]{1,0:T(8,128)(2,1)}, bf16[80,4096]{1,0:T(8,128)(2,1)}, u32[]{:S(2)}, u32[]{:S(2)}) collective-permute-start(bf16[80,4096]{1,0:T(8,128)(2,1)} %constant_dynamic-slice_fusion.1), channel_id=1, source_target_pairs={{0,4},{4,0},{1,5},{5,1},{2,6},{6,2},{3,7},{7,3},{8,12},{12,8},{9,1... | collective-permute-start | bytes 1966088 | tf_op jit(solution)/shard_map/ppermute | solution.py:68
  52.6 17.4 %collective-permute-start.1 = (bf16[128,640]{1,0:T(8,128)(2,1)S(1)}, bf16[128,640]{1,0:T(8,128)(2,1)S(1)}, u32[]{:S(2)}, u32[]{:S(2)}) collective-permute-start(bf16[128,640]{1,0:T(8,128)(2,1)S(1)} %constant_dynamic-slice_fusion.2), channel_id=1, source_target_pairs={{0,4},{4,0},{1,5},{5,1},{2,6},{6,2},{3,7},{7,3},{8,12},{12,8},{9,1... | collective-permute-start | bytes 491528 | tf_op jit(solution)/shard_map/ppermute | solution.py:68
  76.9 117.4 %all-gather.28.cloned.1.call-start = ((), (), s32[]{:S(2)}) async-start(), calls=%async_computation.6 | async-start | bytes 1638400 | tf_op jit(solution)/shard_map/all_gather | solution.py:105
  120.4 10.9 %collective-permute-start.12 = (bf16[2,2,256,640]{3,2,1,0:T(8,128)(2,1)}, bf16[2,2,256,640]{3,2,1,0:T(8,128)(2,1)}, u32[]{:S(2)}, u32[]{:S(2)}) collective-permute-start(bf16[2,2,256,640]{3,2,1,0:T(8,128)(2,1)} %dynamic-slice_bitcast_fusion.1), channel_id=1, source_target_pairs={{0,1},{1,0},{2,3},{3,2},{4,5},{5,4},{6,7},{7,6},{8,9},{9,8},{10,11... | collective-permute-start | bytes 3932168 | tf_op jit(solution)/shard_map/ppermute | solution.py:68
  125.7 24.9 %collective-permute-start.9 = (bf16[2,2,80,4096]{3,2,1,0:T(8,128)(2,1)}, bf16[2,2,80,4096]{3,2,1,0:T(8,128)(2,1)}, u32[]{:S(2)}, u32[]{:S(2)}) collective-permute-start(bf16[2,2,80,4096]{3,2,1,0:T(8,128)(2,1)} %dynamic-slice_bitcast_fusion), channel_id=1, source_target_pairs={{0,1},{1,0},{2,3},{3,2},{4,5},{5,4},{6,7},{7,6},{8,9},{9,8},{10,11... | collective-permute-start | bytes 7864328 | tf_op jit(solution)/shard_map/ppermute | solution.py:68
  126.0 5.3 %copy-start.6 = (bf16[2048,640]{1,0:T(8,128)(2,1)S(1)}, bf16[2048,640]{1,0:T(8,128)(2,1)}, u32[]{:S(2)}) copy-start(bf16[2048,640]{1,0:T(8,128)(2,1)} %copy-done.5) | copy-start | bytes 7864324
  131.2 3.3 copy-start.14
  133.0 17.0 %collective-permute-start.13 = (bf16[2,256,640]{2,1,0:T(8,128)(2,1)S(1)}, bf16[2,256,640]{2,1,0:T(8,128)(2,1)S(1)}, u32[]{:S(2)}, u32[]{:S(2)}) collective-permute-start(bf16[2,256,640]{2,1,0:T(8,128)(2,1)S(1)} %dynamic-slice_bitcast_fusion.3), channel_id=1, source_target_pairs={{0,4},{4,0},{1,5},{5,1},{2,6},{6,2},{3,7},{7,3},{8,12},{12,8},{9,1... | collective-permute-start | bytes 1966088 | tf_op jit(solution)/shard_map/ppermute | solution.py:68
  134.6 16.1 %copy-start.1 = (bf16[640,4096]{1,0:T(8,128)(2,1)S(1)}, bf16[640,4096]{1,0:T(8,128)(2,1)}, u32[]{:S(2)}) copy-start(bf16[640,4096]{1,0:T(8,128)(2,1)} %copy-done) | copy-start | bytes 15728644
  150.2 10.6 %collective-permute-start.14 = (bf16[256,640]{1,0:T(8,128)(2,1)S(1)}, bf16[256,640]{1,0:T(8,128)(2,1)S(1)}, u32[]{:S(2)}, u32[]{:S(2)}) collective-permute-start(bf16[256,640]{1,0:T(8,128)(2,1)S(1)} %dynamic-slice_bitcast_fusion.8), channel_id=1, source_target_pairs={{0,2},{1,3},{2,0},{3,1},{4,6},{5,7},{6,4},{7,5},{8,10},{9,11},{10,... | collective-permute-start | bytes 983048 | tf_op jit(solution)/shard_map/ppermute | solution.py:68
  153.3 3.9 copy-start.3
  154.7 32.8 %collective-permute-start.10 = (bf16[2,80,4096]{2,1,0:T(8,128)(2,1)}, bf16[2,80,4096]{2,1,0:T(8,128)(2,1)}, u32[]{:S(2)}, u32[]{:S(2)}) collective-permute-start(bf16[2,80,4096]{2,1,0:T(8,128)(2,1)} %dynamic-slice_bitcast_fusion.2), channel_id=1, source_target_pairs={{0,2},{1,3},{2,0},{3,1},{4,6},{5,7},{6,4},{7,5},{8,10},{9,11},{10,... | collective-permute-start | bytes 3932168 | tf_op jit(solution)/shard_map/ppermute | solution.py:68
  161.7 103.7 %all-gather.22.cloned.1.call-start = ((), (), s32[]{:S(2)}) async-start(), calls=%async_computation.3 | async-start | bytes 1638400 | tf_op jit(solution)/shard_map/all_gather | solution.py:106
  168.4 78.1 %collective-permute-start.6 = (bf16[2,2,128,640]{3,2,1,0:T(8,128)(2,1)}, bf16[2,2,128,640]{3,2,1,0:T(8,128)(2,1)}, u32[]{:S(2)}, u32[]{:S(2)}) collective-permute-start(bf16[2,2,128,640]{3,2,1,0:T(8,128)(2,1)} %dynamic-slice_bitcast_fusion.5), channel_id=1, source_target_pairs={{0,1},{1,0},{2,3},{3,2},{4,5},{5,4},{6,7},{7,6},{8,9},{9,8},{10,11... | collective-permute-start | bytes 1966088 | tf_op jit(solution)/shard_map/ppermute | solution.py:68
  168.5 19.1 %copy-start.4 = (bf16[2,2,80,4096]{3,2,1,0:T(8,128)(2,1)S(1)}, bf16[2,2,80,4096]{3,2,1,0:T(8,128)(2,1)}, u32[]{:S(2)}) copy-start(bf16[2,2,80,4096]{3,2,1,0:T(8,128)(2,1)} %copy-done.3) | copy-start | bytes 7864324
  196.7 77.9 %all-gather.30.cloned.1.call-start = ((), (), s32[]{:S(2)}) async-start(), calls=%async_computation.7 | async-start | bytes 3276800 | tf_op jit(solution)/shard_map/all_gather | solution.py:105
  199.0 20.2 %collective-permute-start.11 = (bf16[80,4096]{1,0:T(8,128)(2,1)}, bf16[80,4096]{1,0:T(8,128)(2,1)}, u32[]{:S(2)}, u32[]{:S(2)}) collective-permute-start(bf16[80,4096]{1,0:T(8,128)(2,1)} %dynamic-slice_bitcast_fusion.4), channel_id=1, source_target_pairs={{0,4},{4,0},{1,5},{5,1},{2,6},{6,2},{3,7},{7,3},{8,12},{12,8},{9,1... | collective-permute-start | bytes 1966088 | tf_op jit(solution)/shard_map/ppermute | solution.py:68
  221.5 137.1 %all-gather.32.cloned.1.call-start = ((), (), s32[]{:S(2)}) async-start(), calls=%async_computation.8 | async-start | bytes 1474560 | tf_op jit(solution)/shard_map/all_gather | solution.py:105
  223.4 13.0 %copy-start.24 = (f32[256,128]{1,0:T(8,128)S(1)}, f32[256,128]{1,0:T(8,128)}, u32[]{:S(2)}) copy-start(f32[256,128]{1,0:T(8,128)} %copy-done.23) | copy-start | bytes 393220
  223.4 20.3 %collective-permute-start.4 = (bf16[2,256,512]{2,1,0:T(8,128)(2,1)}, bf16[2,256,512]{2,1,0:T(8,128)(2,1)}, u32[]{:S(2)}, u32[]{:S(2)}) collective-permute-start(bf16[2,256,512]{2,1,0:T(8,128)(2,1)} %dynamic-slice_bitcast_fusion.7), channel_id=1, source_target_pairs={{0,1},{1,0},{2,3},{3,2},{4,5},{5,4},{6,7},{7,6},{8,9},{9,8},{10,11... | collective-permute-start | bytes 1572872 | tf_op jit(solution)/shard_map/ppermute | solution.py:68
  245.1 8.7 %collective-permute-start.5 = (bf16[256,512]{1,0:T(8,128)(2,1)S(1)}, bf16[256,512]{1,0:T(8,128)(2,1)S(1)}, u32[]{:S(2)}, u32[]{:S(2)}) collective-permute-start(bf16[256,512]{1,0:T(8,128)(2,1)S(1)} %dynamic-slice_bitcast_fusion.11), channel_id=1, source_target_pairs={{0,2},{1,3},{2,0},{3,1},{4,6},{5,7},{6,4},{7,5},{8,10},{9,11},{10,... | collective-permute-start | bytes 786440 | tf_op jit(solution)/shard_map/ppermute | solution.py:68
  248.6 10.1 %collective-permute-start.7 = (bf16[2,128,640]{2,1,0:T(8,128)(2,1)}, bf16[2,128,640]{2,1,0:T(8,128)(2,1)}, u32[]{:S(2)}, u32[]{:S(2)}) collective-permute-start(bf16[2,128,640]{2,1,0:T(8,128)(2,1)} %dynamic-slice_bitcast_fusion.9), channel_id=1, source_target_pairs={{0,4},{4,0},{1,5},{5,1},{2,6},{6,2},{3,7},{7,3},{8,12},{12,8},{9,1... | collective-permute-start | bytes 983048 | tf_op jit(solution)/shard_map/ppermute | solution.py:68
  253.9 6.5 %copy-start.17 = (bf16[256,4,256]{0,2,1:T(8,128)(2,1)S(1)}, bf16[256,4,256]{0,2,1:T(8,128)(2,1)}, u32[]{:S(2)}) copy-start(bf16[256,4,256]{0,2,1:T(8,128)(2,1)} %copy.118) | copy-start | bytes 1572868
  259.8 5.5 %collective-permute-start.8 = (bf16[128,640]{1,0:T(8,128)(2,1)S(1)}, bf16[128,640]{1,0:T(8,128)(2,1)S(1)}, u32[]{:S(2)}, u32[]{:S(2)}) collective-permute-start(bf16[128,640]{1,0:T(8,128)(2,1)S(1)} %dynamic-slice_bitcast_fusion.12), channel_id=1, source_target_pairs={{0,2},{1,3},{2,0},{3,1},{4,6},{5,7},{6,4},{7,5},{8,10},{9,11},{10,... | collective-permute-start | bytes 491528 | tf_op jit(solution)/shard_map/ppermute | solution.py:68
  260.5 35.2 %copy-start.12 = (bf16[256,1536]{0,1:T(8,128)(2,1)}, bf16[256,1536]{0,1:T(8,128)(2,1)S(1)}, u32[]{:S(2)}) copy-start(bf16[256,1536]{0,1:T(8,128)(2,1)S(1)} %pad_maximum_fusion.16) | copy-start | bytes 2359300
  301.4 2.9 collective-permute-start.15
  304.7 15.4 %collective-permute-start.16 = (bf16[2,96,1536]{2,1,0:T(8,128)(2,1)S(1)}, bf16[2,96,1536]{2,1,0:T(8,128)(2,1)S(1)}, u32[]{:S(2)}, u32[]{:S(2)}) collective-permute-start(bf16[2,96,1536]{2,1,0:T(8,128)(2,1)S(1)} %dynamic-slice_bitcast_fusion.6), channel_id=1, source_target_pairs={{0,4},{4,0},{1,5},{5,1},{2,6},{6,2},{3,7},{7,3},{8,12},{12,8},{9,1... | collective-permute-start | bytes 1769480 | tf_op jit(solution)/shard_map/ppermute | solution.py:68
  320.3 40.6 %copy-start.32 = (bf16[128,640]{1,0:T(8,128)(2,1)S(1)}, bf16[128,640]{1,0:T(8,128)(2,1)}, u32[]{:S(2)}) copy-start(bf16[128,640]{1,0:T(8,128)(2,1)} %reduce_sum.311) | copy-start | bytes 491524
  320.4 8.3 %collective-permute-start.17 = (bf16[96,1536]{1,0:T(8,128)(2,1)S(1)}, bf16[96,1536]{1,0:T(8,128)(2,1)S(1)}, u32[]{:S(2)}, u32[]{:S(2)}) collective-permute-start(bf16[96,1536]{1,0:T(8,128)(2,1)S(1)} %dynamic-slice_bitcast_fusion.10), channel_id=1, source_target_pairs={{0,2},{1,3},{2,0},{3,1},{4,6},{5,7},{6,4},{7,5},{8,10},{9,11},{10,... | collective-permute-start | bytes 884744 | tf_op jit(solution)/shard_map/ppermute | solution.py:68
  329.4 56.1 %all-gather.26.cloned.1.call-start = ((), (), s32[]{:S(2)}) async-start(), calls=%async_computation.5 | async-start | bytes 3276800 | tf_op jit(solution)/shard_map/all_gather | solution.py:106
  330.2 75.0 %all-gather.24.cloned.1.call-start = ((), (), s32[]{:S(2)}) async-start(), calls=%async_computation.4 | async-start | bytes 1474560 | tf_op jit(solution)/shard_map/all_gather | solution.py:106
  358.6 11.4 %copy-start.30 = (f32[256,640]{1,0:T(8,128)S(1)}, f32[256,640]{1,0:T(8,128)}, u32[]{:S(2)}) copy-start(f32[256,640]{1,0:T(8,128)} %get-tuple-element.87) | copy-start | bytes 1966084
  (25 other events, 47.4 us)
Sparse Core Ops, SparseCore 0:
  33.1 16.9 all-gather.15
  52.3 18.1 all-gather.19
  77.1 26.9 all-gather.17
  161.8 32.5 all-gather.27
  196.8 17.2 all-gather.21
  221.6 52.9 all-gather.29
  329.5 29.0 all-gather.31
  360.8 24.7 all-gather.25
  387.7 17.4 all-gather.23
